TPU v7x, 32 devices: a whole 2x2x4 slice. The times are simulated.
32 devices in a mesh: shot: 16 (over z, x, core), coil: 2 (over y).
Axes of the slice: x: 2, y: 2, z: 4, core: 2. Of those that a mesh axis runs over, the one named last changes fastest.
Arguments:
- image: float32 [2, 2, 320, 320], P('coil', None, 'shot'), may hold values from -6 to 6
- sensitivity: bfloat16 [4, 2, 2, 320, 320], P('coil'), may hold values from -3 to 3
- warp_table: bfloat16 [16, 2, 128, 128], P('shot')
- warp_source: int32 [16, 800, 2], P('shot'), may hold values from 0 to 799
- warp_live: int32 [16, 800, 2], P('shot'), may hold values 0 or 1
- sampled_lines: int32 [16, 20], P('shot'), may hold values from 0 to 319, as said below
- measured: float32 [16, 4, 2, 20, 640], P('shot', 'coil'), may hold values from -6 to 6
Outputs:
- image_out: float32 [2, 2, 320, 320], P('coil', None, 'shot')
- residual_out: float32 [16, 4, 2, 20, 640], P('shot', 'coil')
Inputs may be any that keep to these rules, and one draw needn't show every extreme that they name: `sampled_lines`: taken together, the shots acquire each of the 320 phase-encode lines exactly once.
All inputs are finite; a program needn't handle non-finite values. No bound on the sum of `warp_live` on one device may be relied on, other than what follows from the above.
Results may differ from a plain program's by a relative error of at most 0.017.
Values may be sent and summed in bfloat16 or wider, within the bound.
No kernel may reach another device: no remote copies, remote signals or barrier semaphores. Data moves between devices by JAX's collectives and lax.ppermute only.
A program may use at most 128 MiB of HBM per device.

v0:
```python
import functools
import math

import jax
import jax.numpy as jnp
import numpy as np
from jax import lax
from jax.experimental import pallas as pl
from jax.experimental.pallas import tpu as pltpu
from jax.sharding import PartitionSpec as P


BF = jnp.bfloat16
F32 = jnp.float32
AXES = ("shot", "coil")


def round_up(value, unit):
    return -(-value // unit) * unit


def dft_tables(rows, cols):
    def parts(length):
        index = np.arange(length, dtype=np.int64)
        angle = (index[:, None] * index[None, :] % length) * (-2.0 * math.pi / length)
        return np.cos(angle) / math.sqrt(length), np.sin(angle) / math.sqrt(length)

    real, imag = parts(cols)
    readout = np.block([[real, imag], [-imag, real]])
    real, imag = parts(rows)
    lines = []
    for odd in (0, 1):
        re, im = real[:, odd::2], imag[:, odd::2]
        lines.append(np.concatenate([re, -im], axis=1).T)
        lines.append(np.concatenate([im, re], axis=1).T)
    as_bf = lambda t: t.astype(np.float32).astype(jnp.bfloat16)
    return as_bf(readout), as_bf(np.stack(lines))


def dot(left, right):
    return jnp.dot(left, right, preferred_element_type=F32)


def dot_nt(left, right):
    return lax.dot_general(left, right, (((1,), (1,)), ((), ())), preferred_element_type=F32)


def call(body, out_shape, slices, scratch=(), smem=0, far=0):
    def run(*args):
        near = len(args) - smem - far
        specs = [pl.BlockSpec(memory_space=pltpu.SMEM)] * smem
        specs += [pl.BlockSpec(memory_space=pltpu.VMEM)] * near
        specs += [pl.BlockSpec(memory_space=pl.ANY)] * far
        args = list(args[: smem + near]) + [
            pltpu.with_memory_space_constraint(arg, pltpu.HBM) for arg in args[smem + near :]
        ]
        return pl.pallas_call(
            body,
            out_shape=out_shape,
            in_specs=specs,
            out_specs=jax.tree.map(lambda _: pl.BlockSpec(memory_space=pltpu.VMEM), out_shape),
            scratch_shapes=list(scratch),
            compiler_params=pltpu.CompilerParams(
                vmem_limit_bytes=min(8 + 6 * slices, 56) * 1024 * 1024
            ),
        )(*args)

    return run


def fetch(pairs, sems):
    copies = [pltpu.make_async_copy(a, b, sems.at[i]) for i, (a, b) in enumerate(pairs)]
    for copy in copies:
        copy.start()
    return copies


def wanted_of(source_far, live_far, source, live, sems):
    for copy in fetch([(source_far, source), (live_far, live)], sems):
        copy.wait()
    return jnp.where(live[...] != 0, source[...], -1)


def spread_body(slots, source_far, live_far, spread, source, live, wanted, sems):
    blocks, wide = spread.shape
    table = wanted_of(source_far, live_far, source, live, sems)
    for k in range(wide // blocks):
        wanted[:, k * blocks : (k + 1) * blocks] = table[k : k + 1, :]
    down = lax.broadcasted_iota(jnp.int32, (blocks, wide), 0)
    spread[...] = jnp.where(down == jnp.broadcast_to(wanted[...], (blocks, wide)), 1.0, 0.0).astype(BF)


def pick_body(slots, source_far, live_far, pick, source, live, sems):
    members, blocks, _ = pick.shape
    table = wanted_of(source_far, live_far, source, live, sems)
    full = round_up(blocks, 128)
    along = lax.broadcasted_iota(jnp.int32, (blocks, blocks), 1).astype(F32)
    for k in range(members):
        flat = jnp.broadcast_to(table[k : k + 1, :], (8, blocks)).astype(F32)
        if full > blocks:
            flat = jnp.concatenate([flat, jnp.zeros((8, full - blocks), F32)], axis=1)
        by_row = flat.T[:blocks, :1]
        pick[k] = jnp.where(along == by_row, 1.0, 0.0).astype(BF)


def tables_body(*refs, coils, kept):
    maps_far, lines_far, line_tables_far, *refs = refs
    kept_far, refs = refs[:kept], refs[kept:]
    rows_out, cols_out, *refs = refs
    sens, kept_out, refs = refs[:coils], refs[coils : coils + kept], refs[coils + kept :]
    maps, lines, line_tables, padded, wide, sems = refs
    first, second, third, *rest = fetch(
        [(maps_far, maps), (line_tables_far, line_tables), (lines_far, lines), *zip(kept_far, kept_out)],
        sems,
    )
    first.wait()
    for c in range(coils):
        pair_body(maps, c, sens[c], wide)
    second.wait()
    third.wait()
    lines_body(lines, line_tables, rows_out, cols_out, padded)
    for copy in rest:
        copy.wait()


def lines_body(lines, tables, rows_out, cols_out, padded):
    lp = rows_out.shape[0] // 4
    count = tables.shape[2]
    padded[...] = jnp.full(padded.shape, -1, jnp.int32)
    padded[:, : lines.shape[1]] = lines[...]
    wide = jnp.broadcast_to(padded[:, :lp], (count, lp))
    chosen = jnp.where(lax.broadcasted_iota(jnp.int32, (count, lp), 0) == wide, 1.0, 0.0).astype(BF)
    eye = lax.broadcasted_iota(jnp.int32, (lp, lp), 0) == lax.broadcasted_iota(jnp.int32, (lp, lp), 1)
    eye = jnp.where(eye, 1.0, 0.0).astype(BF)
    for part in range(4):
        got = dot(tables[part], chosen).astype(BF)
        cols_out[:, part * lp : (part + 1) * lp] = got
        rows_out[part * lp : (part + 1) * lp, :] = dot_nt(eye, got).astype(BF)


def pair_body(maps, coil, out, wide):
    count, rows, cols = maps.shape[1:]
    half = rows // 2
    low = lax.broadcasted_iota(jnp.int32, (half, 2 * cols), 1) < cols
    width = wide.shape[2]
    used = range(0, cols, width)
    spare = [jnp.zeros((half, 2 * cols - width * len(used)), F32)]
    for i in range(count):
        for t, start in enumerate(used):
            stop = min(start + width, cols)
            wide[t, :, : stop - start] = maps[coil, i, :, start:stop].astype(F32)
        even, odd = (
            jnp.concatenate([wide[t, pl.ds(e, half, stride=2), :] for t in range(len(used))] + spare, axis=1)
            for e in range(2)
        )
        out[i] = jnp.where(low, even, pltpu.roll(odd, cols, 1)).astype(BF)


def halves_dot(left, right):
    half = left.shape[0] // 2
    return jnp.concatenate([dot(left[:half, :], right), dot(left[half:, :], right)], axis=0)


def warp(volume, pick, kernels, width):
    members = kernels.shape[0]
    picked = [dot(pick[k], volume).astype(BF) for k in range(members)]
    table = jnp.concatenate([kernels[k] for k in range(members)], axis=0)
    planes = []
    for e in range(2):
        cut = slice(e * width, (e + 1) * width)
        planes.append(dot(jnp.concatenate([p[:, cut] for p in picked], axis=1), table))
    return jnp.concatenate(planes, axis=1)


def unwarp(planes, spread, kernels):
    members = kernels.shape[0]
    rows = [
        jnp.concatenate([dot_nt(plane, kernels[k]) for plane in planes], axis=1).astype(BF)
        for k in range(members)
    ]
    return halves_dot(spread, jnp.concatenate(rows, axis=0)).astype(BF)


def pairs_of(ref, plane, rows, tiles):
    return jnp.concatenate([ref[plane, pl.ds(j, rows, stride=tiles), :] for j in range(tiles)], axis=1)


def coil_rows(warped, at, sens, z, rows_table, place, lines):
    width = warped.shape[2]
    half, wide = sens[0].shape[1], sens[0].shape[2]
    cols = wide // 2
    tiles = wide // width
    lp = rows_table.shape[0] // 4
    real = pairs_of(warped, at, half, tiles).astype(BF)
    imag = pairs_of(warped, at + 1, half, tiles).astype(BF)
    low = lax.broadcasted_iota(jnp.int32, (lp, wide), 1) < cols
    for c, maps in enumerate(sens):
        sr, si = maps[2 * z], maps[2 * z + 1]
        coil = jnp.concatenate([sr * real - si * imag, sr * imag + si * real], axis=0)
        found = dot(rows_table[...], coil)
        stay = jnp.where(low, found[:lp], found[3 * lp :])
        move = jnp.where(low, found[lp : 2 * lp], found[2 * lp : 3 * lp])
        lines[place(c)] = (stay + pltpu.roll(move, cols, 1)).astype(BF)


def readout_of(lines, readout):
    batch, lp, wide = lines.shape
    return dot(lines[...].reshape(batch * lp, wide), readout[...])


def plane_at(slots, position, planes):
    half = planes // 2
    return position ^ slots[0] if position < half else (position - half) ^ slots[2]


def put_halves(target, at, turn, planes):
    rows, width = planes.shape[0] // 2, planes.shape[1] // 2
    for e in range(2):
        for h in range(2):
            target[at + e, h ^ turn] = planes[h * rows : (h + 1) * rows, e * width : (e + 1) * width]


def first_body(slots, mine, other, pick, spread, kernels, *refs, slab, coils, slices, shots, coil_parts):
    sens, refs = refs[:coils], refs[coils:]
    rows_table, cols_table, readout, measured, residual, send, rest, pieces, volume, warped, lines = refs
    width = warped.shape[2]
    half, wide = sens[0].shape[1], sens[0].shape[2]
    cols = wide // 2
    tiles = wide // width
    lp = rows_table.shape[0] // 4
    count = measured.shape[1]
    per_part = slices // coil_parts
    own = mine.shape[0]
    pieces[:own] = mine[...]
    pieces[own:] = other[...]
    for z in range(slices):
        part, inner = z // per_part, z % per_part
        for s in range(shots):
            piece = pieces[slots[6 + s * coil_parts + part]].astype(F32)
            for plane in range(2):
                start = (inner * 2 + plane) * slab
                volume[z, s * slab : (s + 1) * slab, plane * width : (plane + 1) * width] = piece[
                    start : start + slab
                ]
        moved = warp(volume[z].astype(BF), pick, kernels, width)
        for plane in range(2):
            moved_plane = moved[:, plane * width : (plane + 1) * width]
            warped[2 * z + plane] = moved_plane.astype(BF).astype(F32)
        coil_rows(warped, 2 * z, sens, z, rows_table, lambda c, z=z: c * slices + z, lines)
    spectrum = readout_of(lines, readout)
    for c in range(coils):
        for z in range(slices):
            i = c * slices + z
            left = spectrum[i * lp : i * lp + count] - measured[c, :, z, :]
            residual[c, :, z, :] = left
            if count < lp:
                left = jnp.concatenate([left, jnp.zeros((lp - count, wide), F32)], axis=0)
            lines[i] = left.astype(BF)
    back = dot_nt(lines[...].reshape(coils * slices * lp, wide), readout[...])
    low = lax.broadcasted_iota(jnp.int32, (lp, wide), 1) < cols
    zero = jnp.zeros((lp, wide), F32)
    for z in range(slices):
        real, imag = None, None
        for c in range(coils):
            i = c * slices + z
            rows = back[i * lp : (i + 1) * lp]
            turned = pltpu.roll(rows, cols, 1)
            spreadout = jnp.concatenate(
                [
                    jnp.where(low, rows, zero),
                    jnp.where(low, turned, zero),
                    jnp.where(low, zero, turned),
                    jnp.where(low, zero, rows),
                ],
                axis=0,
            ).astype(BF)
            got = dot(cols_table[...], spreadout).astype(BF)
            gr, gi = got[:half], got[half:]
            sr, si = sens[c][2 * z], sens[c][2 * z + 1]
            more_real, more_imag = sr * gr + si * gi, sr * gi - si * gr
            real = more_real if real is None else real + more_real
            imag = more_imag if imag is None else imag + more_imag
        for j in range(tiles):
            cut = slice(j * width, (j + 1) * width)
            warped[2 * z, pl.ds(j, half, stride=tiles), :] = real[:, cut].astype(F32)
            warped[2 * z + 1, pl.ds(j, half, stride=tiles), :] = imag[:, cut].astype(F32)
    planes = 2 * slices
    for at in range(0, planes // 2, 2):
        chosen = [warped[plane_at(slots, planes // 2 + at + e, planes)].astype(BF) for e in range(2)]
        put_halves(send, at, slots[3], unwarp(chosen, spread, kernels))
    for at in range(planes // 2):
        rest[at] = warped[plane_at(slots, at, planes)].astype(BF)


def keep_body(slots, rest, spread, kernels, keep):
    for at in range(0, rest.shape[0], 2):
        put_halves(keep, at, slots[1], unwarp([rest[at], rest[at + 1]], spread, kernels))


def forward_part(slots, start, source, pick, kernels, sens, rows_table, lines, bands, volume, warped, *, slab):
    half_planes = source.shape[0]
    planes = 2 * half_planes
    blocks, width = warped.shape[1], warped.shape[2]
    rows = blocks // 2
    turn = slots[1] if start == 0 else slots[3]
    slab_rows = bands.shape[1]
    at_row = lax.broadcasted_iota(jnp.int32, (slab_rows, blocks), 0) + slots[4] * slab
    mine = jnp.where(lax.broadcasted_iota(jnp.int32, (slab_rows, blocks), 1) == at_row, 1.0, 0.0).astype(BF)
    square = jnp.zeros((8, 2 * width), F32)
    for at in range(0, half_planes, 2):
        for e in range(2):
            for h in range(2):
                volume[h * rows : (h + 1) * rows, e * width : (e + 1) * width] = source[at + e, h ^ turn]
        value = volume[...]
        as_f32 = value.astype(F32)
        square = square + jnp.sum((as_f32 * as_f32).reshape(blocks // 8, 8, 2 * width), axis=0)
        band = dot(mine, value)
        moved = warp(value, pick, kernels, width)
        for e in range(2):
            plane = plane_at(slots, start + at + e, planes)
            cut = slice(e * width, (e + 1) * width)
            warped[plane & 1] = moved[:, cut].astype(BF).astype(F32)
            bands[at + e] = band[:, cut]
        z = plane_at(slots, start + at, planes) >> 1
        coil_rows(warped, 0, sens, z, rows_table, lambda c, at=at: c * (half_planes // 2) + at // 2, lines)
    return square


def near_body(slots, near, pick, kernels, *refs, slab, coils):
    sens, refs = refs[:coils], refs[coils:]
    rows_table, lines, bands, square, volume, warped = refs
    square[...] = forward_part(
        slots, 0, near, pick, kernels, sens, rows_table, lines, bands, volume, warped, slab=slab
    )


def second_body(slots, far, near_lines, near_bands, near_square, pick, kernels, *refs, slab, coils):
    sens, refs = refs[:coils], refs[coils:]
    rows_table, readout, spectrum, sums, norm, own_rows, *refs = refs
    volume, warped, far_lines, far_bands, lines, bands = refs
    half_planes = far.shape[0]
    planes = 2 * half_planes
    slices = half_planes
    width = warped.shape[2]
    wide = sens[0].shape[2]
    cols = wide // 2
    tiles = wide // width
    lp = rows_table.shape[0] // 4
    count = spectrum.shape[1]
    coil = slots[5]
    square = near_square[...] + forward_part(
        slots, half_planes, far, pick, kernels, sens, rows_table, far_lines, far_bands, volume, warped,
        slab=slab,
    )
    for start, some_lines, some_bands in ((0, near_lines, near_bands), (half_planes, far_lines, far_bands)):
        for at in range(half_planes):
            bands[plane_at(slots, start + at, planes)] = some_bands[at]
        for at in range(0, half_planes, 2):
            z = plane_at(slots, start + at, planes) >> 1
            for c in range(coils):
                lines[c * slices + z] = some_lines[c * (slices // 2) + at // 2]
    found = readout_of(lines, readout)
    sums[...] = jnp.broadcast_to(jnp.sum(found * found), sums.shape)
    norm[...] = jnp.broadcast_to(jnp.sum(square), norm.shape)
    for c in range(coils):
        for z in range(slices):
            i = c * slices + z
            spectrum[c, :, z, :] = found[i * lp : i * lp + count]
    own = own_rows.shape[0]
    pairs = own_rows.shape[1] // 2
    for i in range(own):
        for plane in range(2):
            got = pairs_of(bands, (coil * own + i) * 2 + plane, pairs, tiles)
            turned = pltpu.roll(got, cols, 1)
            for r in range(pairs):
                own_rows[i, 2 * r, plane, :] = got[r, :cols]
                own_rows[i, 2 * r + 1, plane, :] = turned[r, :cols]


def last_body(totals, norm, image, own, residual, spectrum, image_out, residual_out):
    image_norm = jnp.sum(totals[:, :1])
    step = norm[:, :1] / (image_norm + 1e-06)
    image_out[...] = image[...] - step[0, 0] * own[...]
    residual_out[...] = residual[...] - step[0, 0] * spectrum[...]


def exchange_pairs(partner, shots, coils):
    pairs = []
    for s in range(shots):
        for c in range(coils):
            t, d = partner(s, c)
            pairs.append((s * coils + c, t * coils + d))
    return pairs


def slot_table(shots, coil_parts, planes):
    shot_bits, coil_bits = range(2, shots.bit_length() - 1), range(1, coil_parts.bit_length() - 1)
    table = []
    for shot in range(shots):
        for coil in range(coil_parts):
            ways = ((shot >> 1) & 1, coil & 1)
            a, b = (ways[1], ways[0]) if shot % 2 == 0 else ways
            row = [
                (shot & 1) * (planes // 2) + a * (planes // 4), b,
                (1 - (shot & 1)) * (planes // 2) + b * (planes // 4), a, shot, coil,
            ]
            for s in range(shots):
                for c in range(coil_parts):
                    ds, dc = s ^ shot, c ^ coil
                    rest = [(ds >> i) & 1 for i in shot_bits] + [(dc >> i) & 1 for i in coil_bits]
                    one, two = (ds >> 1) & 1, dc & 1
                    bits = rest[::-1] + ([one, two] if s % 2 == 0 else [two, one]) + [ds & 1]
                    row.append(sum(bit << i for i, bit in enumerate(bits)))
            table.append(row)
    return np.array(table, np.int32)


def shards(shots, coil_parts, image, sensitivity, warp_table, warp_source, warp_live, sampled_lines, measured):
    coils, slices, _, rows, cols = sensitivity.shape
    members, width = warp_table.shape[1], warp_table.shape[2]
    blocks = warp_source.shape[1]
    count = sampled_lines.shape[1]
    lp = round_up(count, 16)
    own_slices = image.shape[0]
    slab = blocks // shots
    planes = 2 * slices

    core = lambda s, c: (s ^ 1, c)
    by_shot = lambda s, c: (s ^ 2, c)
    by_coil = lambda s, c: (s, c ^ 1)
    first_way = lambda s, c: by_coil(s, c) if s & 1 == 0 else by_shot(s, c)
    second_way = lambda s, c: by_shot(s, c) if s & 1 == 0 else by_coil(s, c)
    rest = [lambda s, c, b=b: (s ^ b, c) for b in (1 << i for i in range(2, shots.bit_length() - 1))]
    rest += [lambda s, c, b=b: (s, c ^ b) for b in (1 << i for i in range(1, coil_parts.bit_length() - 1))]

    def swap(value, partner):
        return lax.ppermute(value, AXES, exchange_pairs(partner, shots, coil_parts))

    piece = image.astype(BF).reshape(1, own_slices * 2 * slab, width)
    for i in reversed(range(len(rest))):
        got = swap(piece, rest[i])
        piece = jnp.concatenate([piece, got], axis=0)
    second = swap(piece, second_way)
    early = swap(piece, first_way)
    late = swap(second, first_way)
    piece = jnp.concatenate([piece, second, early, late], axis=0)
    other = swap(piece, core)

    table = slot_table(shots, coil_parts, planes)
    slots = lax.dynamic_slice(
        jnp.asarray(table), (lax.axis_index(AXES), 0), (1, table.shape[1]), allow_negative_indices=False
    )[0]
    readout_np, lines_np = dft_tables(rows, cols)
    readout, line_tables = jnp.asarray(readout_np), jnp.asarray(lines_np)
    kernels = warp_table[0]
    shape = jax.ShapeDtypeStruct
    vmem = lambda value: pltpu.VMEM(value.shape, value.dtype)
    source, live = warp_source[0].T, warp_live[0].T
    both = [vmem(source), vmem(live)]
    sems = pltpu.SemaphoreType.DMA((2,))
    spread = call(
        spread_body, shape((blocks, members * blocks), BF), slices,
        scratch=both + [pltpu.VMEM((1, members * blocks), jnp.int32), sems], smem=1, far=2,
    )(slots, source, live)
    pick = call(
        pick_body, shape((members, blocks, blocks), BF), slices, scratch=both + [sems], smem=1, far=2,
    )(slots, source, live)
    seen = measured[0].transpose(0, 2, 1, 3)
    rows_first = image.transpose(0, 2, 1, 3)
    kept = [readout, kernels, seen, rows_first]
    maps = sensitivity.reshape(coils, 2 * slices, rows, cols)
    rows_table, cols_table, *refs = call(
        functools.partial(tables_body, coils=coils, kept=len(kept)),
        [shape((4 * lp, rows), BF), shape((rows, 4 * lp), BF)]
        + [shape((2 * slices, rows // 2, 2 * cols), BF)] * coils
        + [shape(value.shape, value.dtype) for value in kept],
        slices,
        scratch=[
            vmem(maps), vmem(sampled_lines), vmem(line_tables), pltpu.VMEM((1, 128), jnp.int32),
            pltpu.VMEM((-(-cols // width), rows, width), F32),
            pltpu.SemaphoreType.DMA((3 + len(kept),)),
        ],
        far=3 + len(kept),
    )(maps, sampled_lines, line_tables, *kept)
    sens, (readout, kernels, seen, rows_first) = refs[:coils], refs[coils:]
    sizes = dict(slab=slab, coils=coils)
    batch = coils * slices
    shaped = shape((planes // 2, 2, blocks // 2, width), BF)
    residual, send, rest_planes = call(
        functools.partial(first_body, slices=slices, shots=shots, coil_parts=coil_parts, **sizes),
        [shape(seen.shape, F32), shaped, shape((planes // 2, blocks, width), BF)],
        slices,
        scratch=[
            pltpu.VMEM((shots * coil_parts,) + piece.shape[1:], BF),
            pltpu.VMEM((slices, blocks, 2 * width), F32),
            pltpu.VMEM((planes, blocks, width), F32),
            pltpu.VMEM((batch, lp, 2 * cols), BF),
        ],
        smem=1,
    )(slots, piece, other, pick, spread, kernels, *sens, rows_table, cols_table, readout, seen)
    got = swap(send, core)
    keep = call(keep_body, shaped, slices, smem=1)(slots, rest_planes, spread, kernels)

    def add(left, right):
        return (left.astype(F32) + right.astype(F32)).astype(BF)

    quarter = planes // 4
    out2, stay2 = add(keep[quarter:], got[quarter:]), add(keep[:quarter], got[:quarter])
    got = swap(out2[:, 1], first_way)
    stay_got = swap(out2[:, 0], first_way)
    out3, total = add(stay2[:, 1], got), add(stay2[:, 0], stay_got)
    got = swap(out3, second_way)
    total = add(total, got)
    for partner in rest:
        total = add(total, swap(total, partner))
    second = swap(total, second_way)
    early = swap(total, first_way)
    late = swap(second, first_way)
    near = jnp.concatenate(
        [jnp.stack([total, second], axis=1), jnp.stack([early, late], axis=1)], axis=0
    )
    far = swap(near, core)

    devices = shots * coil_parts
    slab_rows = round_up(slab, 16)
    work = [pltpu.VMEM((blocks, 2 * width), BF), pltpu.VMEM((2, blocks, width), F32)]
    lines_half, bands_half = (batch // 2, lp, 2 * cols), (planes // 2, slab_rows, width)
    near_lines, near_bands, near_square = call(
        functools.partial(near_body, **sizes),
        [shape(lines_half, BF), shape(bands_half, F32), shape((8, 2 * width), F32)],
        slices, scratch=work, smem=1,
    )(slots, near, pick, kernels, *sens, rows_table)
    spectrum, sums, norm, own = call(
        functools.partial(second_body, **sizes),
        [
            shape(seen.shape, F32),
            shape((devices, 128), F32),
            shape((1, 128), F32),
            shape((own_slices, image.shape[2], 2, cols), F32),
        ],
        slices,
        scratch=work
        + [
            pltpu.VMEM(lines_half, BF),
            pltpu.VMEM(bands_half, F32),
            pltpu.VMEM((batch, lp, 2 * cols), BF),
            pltpu.VMEM((planes, slab_rows, width), F32),
        ],
        smem=1,
    )(slots, far, near_lines, near_bands, near_square, pick, kernels, *sens, rows_table, readout)
    totals = lax.all_to_all(sums, AXES, 0, 0, tiled=True)
    image, residual = call(
        last_body, [shape(rows_first.shape, F32), shape(seen.shape, F32)], slices
    )(totals, norm, rows_first, own, residual, spectrum)
    return image.transpose(0, 2, 1, 3), residual.transpose(0, 2, 1, 3)[None]


def solution(mesh):
    def body(*args):
        return shards(mesh.shape["shot"], mesh.shape["coil"], *args)

    return jax.shard_map(
        body,
        mesh=mesh,
        in_specs=(
            P("coil", None, "shot", None),
            P("coil", None, None, None, None),
            P("shot", None, None, None),
            P("shot", None, None),
            P("shot", None, None),
            P("shot", None),
            P("shot", "coil", None, None, None),
        ),
        out_specs=(P("coil", None, "shot", None), P("shot", "coil", None, None, None)),
        check_vma=False,
    )
```

profile of v0, /device:TPU:0, one launch (start us, length us, event | category | flops | bytes accessed | tf_op | source)
XLA Modules:
  0.0 90.1 jit_solution(10872590190591118557)
XLA Ops:
  1.6 4.1 %collective-permute-start = (bf16[1,100,128]{2,1,0:T(8,128)(2,1)S(1)}, bf16[1,100,128]{2,1,0:T(8,128)(2,1)S(1)}, u32[]{:S(2)}, u32[]{:S(2)}) collective-permute-start(bf16[1,100,128]{2,1,0:T(8,128)(2,1)S(1)} %reshape.40), channel_id=1, source_target_pairs={{0,16},{1,17},{2,18},{3,19},{4,20},{5,21},{6,22},{7,23},{8,24},{9,... | collective-permute-start | bytes 76808 | tf_op jit(solution)/shard_map/ppermute | solution.py:437
  5.7 1.8 %collective-permute-done = bf16[1,100,128]{2,1,0:T(8,128)(2,1)S(1)} collective-permute-done((bf16[1,100,128]{2,1,0:T(8,128)(2,1)S(1)}, bf16[1,100,128]{2,1,0:T(8,128)(2,1)S(1)}, u32[]{:S(2)}, u32[]{:S(2)}) %collective-permute-start) | collective-permute-done | bytes 25632 | tf_op jit(solution)/shard_map/ppermute | solution.py:437
  7.6 2.0 %collective-permute-start.1 = (bf16[2,100,128]{2,1,0:T(8,128)(2,1)S(1)}, bf16[2,100,128]{2,1,0:T(8,128)(2,1)S(1)}, u32[]{:S(2)}, u32[]{:S(2)}) collective-permute-start(bf16[2,100,128]{2,1,0:T(8,128)(2,1)S(1)} %pad_maximum_fusion), channel_id=1, source_target_pairs={{0,8},{1,9},{2,10},{3,11},{4,12},{5,13},{6,14},{7,15},{8,0},{9,1},... | collective-permute-start | bytes 153608 | tf_op jit(solution)/shard_map/ppermute | solution.py:437
  9.6 2.2 %collective-permute-done.1 = bf16[2,100,128]{2,1,0:T(8,128)(2,1)S(1)} collective-permute-done((bf16[2,100,128]{2,1,0:T(8,128)(2,1)S(1)}, bf16[2,100,128]{2,1,0:T(8,128)(2,1)S(1)}, u32[]{:S(2)}, u32[]{:S(2)}) %collective-permute-start.1) | collective-permute-done | bytes 51232 | tf_op jit(solution)/shard_map/ppermute | solution.py:437
  11.8 2.0 %collective-permute-start.2 = (bf16[4,100,128]{2,1,0:T(8,128)(2,1)S(1)}, bf16[4,100,128]{2,1,0:T(8,128)(2,1)S(1)}, u32[]{:S(2)}, u32[]{:S(2)}) collective-permute-start(bf16[4,100,128]{2,1,0:T(8,128)(2,1)S(1)} %get-tuple-element.46), channel_id=1, source_target_pairs={{0,4},{1,5},{2,3},{3,2},{4,0},{5,1},{6,7},{7,6},{8,12},{9,13},{10,... | collective-permute-start | bytes 307208 | tf_op jit(solution)/shard_map/ppermute | solution.py:437
  15.4 2.0 %collective-permute-done.2 = bf16[4,100,128]{2,1,0:T(8,128)(2,1)S(1)} collective-permute-done((bf16[4,100,128]{2,1,0:T(8,128)(2,1)S(1)}, bf16[4,100,128]{2,1,0:T(8,128)(2,1)S(1)}, u32[]{:S(2)}, u32[]{:S(2)}) %collective-permute-start.2) | collective-permute-done | bytes 102432 | tf_op jit(solution)/shard_map/ppermute | solution.py:437
  17.3 2.4 %collective-permute-start.4 = (bf16[4,100,128]{2,1,0:T(8,128)(2,1)S(1)}, bf16[4,100,128]{2,1,0:T(8,128)(2,1)S(1)}, u32[]{:S(2)}, u32[]{:S(2)}) collective-permute-start(bf16[4,100,128]{2,1,0:T(8,128)(2,1)S(1)} %collective-permute-done.2), channel_id=1, source_target_pairs={{0,1},{1,0},{2,6},{3,7},{4,5},{5,4},{6,2},{7,3},{8,9},{9,8},{10,14... | collective-permute-start | bytes 307208 | tf_op jit(solution)/shard_map/ppermute | solution.py:437
  19.7 2.6 %collective-permute-done.4 = bf16[4,100,128]{2,1,0:T(8,128)(2,1)S(1)} collective-permute-done((bf16[4,100,128]{2,1,0:T(8,128)(2,1)S(1)}, bf16[4,100,128]{2,1,0:T(8,128)(2,1)S(1)}, u32[]{:S(2)}, u32[]{:S(2)}) %collective-permute-start.4) | collective-permute-done | bytes 102432 | tf_op jit(solution)/shard_map/ppermute | solution.py:437
  23.2 2.5 %shard_map.114.spread = bf16[800,1600]{1,0:T(8,128)(2,1)S(1)} custom-call(s32[38]{0:T(128)S(1)} %dynamic-slice_bitcast_fusion.slots, s32[2,800]{1,0:T(2,128)} %bitcast.50, s32[2,800]{1,0:T(2,128)} %bitcast.52), custom_call_target="tpu_custom_call" | custom-call | tf_op jit(solution)/shard_map/pallas_call | solution.py:57
  25.7 2.1 %shard_map.113.pick = bf16[2,800,800]{2,1,0:T(8,128)(2,1)S(1)} custom-call(s32[38]{0:T(128)S(1)} %dynamic-slice_bitcast_fusion.slots, s32[2,800]{1,0:T(2,128)} %bitcast.51, s32[2,800]{1,0:T(2,128)} %bitcast.53), custom_call_target="tpu_custom_call" | custom-call | tf_op jit(solution)/shard_map/pallas_call | solution.py:57
  27.8 3.3 %shard_map.115 = (bf16[128,320]{1,0:T(8,128)(2,1)S(1)}, bf16[320,128]{1,0:T(8,128)(2,1)S(1)}, bf16[4,160,640]{2,1,0:T(8,128)(2,1)S(1)}, bf16[4,160,640]{2,1,0:T(...) custom-call(bf16[2,4,320,320]{3,2,1,0:T(8,128)(2,1)} %bitcast.42, ...), custom_call_target="tpu_custom_call" | custom-call | tf_op jit(solution)/shard_map/pallas_call | solution.py:57
  31.1 6.2 %shard_map.116 = (f32[2,20,2,640]{3,2,1,0:T(2,128)S(1)}, bf16[2,2,400,128]{3,2,1,0:T(8,128)(2,1)S(1)}, bf16[2,800,128]{2,1,0:T(8,128)(2,1)S(1)}) custom-call(s32[38]{0:T(128)S(1)} %dynamic-slice_bitcast_fusion.slots, bf16[16,100,128]{2,1,0:T(8,128)(2,1)S(1)} %constant_dynamic-update-slice_fusion.3.mine, ...), custom_call_target="tpu_custom_call" | custom-call | tf_op jit(solution)/shard_map/pallas_call | solution.py:57
  39.6 2.1 %collective-permute-start.8 = (bf16[1,400,128]{2,1,0:T(8,128)(2,1)S(1)}, bf16[1,400,128]{2,1,0:T(8,128)(2,1)S(1)}, u32[]{:S(2)}, u32[]{:S(2)}) collective-permute-start(bf16[1,400,128]{2,1,0:T(8,128)(2,1)S(1)} %get-tuple-element.45), channel_id=1, source_target_pairs={{0,1},{1,0},{2,6},{3,7},{4,5},{5,4},{6,2},{7,3},{8,9},{9,8},{10,14... | collective-permute-start | bytes 307208 | tf_op jit(solution)/shard_map/ppermute | solution.py:437
  41.8 2.6 %collective-permute-done.8 = bf16[1,400,128]{2,1,0:T(8,128)(2,1)S(1)} collective-permute-done((bf16[1,400,128]{2,1,0:T(8,128)(2,1)S(1)}, bf16[1,400,128]{2,1,0:T(8,128)(2,1)S(1)}, u32[]{:S(2)}, u32[]{:S(2)}) %collective-permute-start.8) | collective-permute-done | bytes 102432 | tf_op jit(solution)/shard_map/ppermute | solution.py:437
  44.4 2.1 %collective-permute-start.9 = (bf16[1,400,128]{2,1,0:T(8,128)(2,1)S(1)}, bf16[1,400,128]{2,1,0:T(8,128)(2,1)S(1)}, u32[]{:S(2)}, u32[]{:S(2)}) collective-permute-start(bf16[1,400,128]{2,1,0:T(8,128)(2,1)S(1)} %fusion), channel_id=1, source_target_pairs={{0,4},{1,5},{2,3},{3,2},{4,0},{5,1},{6,7},{7,6},{8,12},{9,13},{10,... | collective-permute-start | bytes 307208 | tf_op jit(solution)/shard_map/ppermute | solution.py:437
  46.4 2.7 %collective-permute-done.9 = bf16[1,400,128]{2,1,0:T(8,128)(2,1)S(1)} collective-permute-done((bf16[1,400,128]{2,1,0:T(8,128)(2,1)S(1)}, bf16[1,400,128]{2,1,0:T(8,128)(2,1)S(1)}, u32[]{:S(2)}, u32[]{:S(2)}) %collective-permute-start.9) | collective-permute-done | bytes 102432 | tf_op jit(solution)/shard_map/ppermute | solution.py:437
  49.2 1.8 %collective-permute-start.10 = (bf16[1,400,128]{2,1,0:T(8,128)(2,1)S(1)}, bf16[1,400,128]{2,1,0:T(8,128)(2,1)S(1)}, u32[]{:S(2)}, u32[]{:S(2)}) collective-permute-start(bf16[1,400,128]{2,1,0:T(8,128)(2,1)S(1)} %add_convert_fusion.4), channel_id=1, source_target_pairs={{0,8},{1,9},{2,10},{3,11},{4,12},{5,13},{6,14},{7,15},{8,0},{9,1},... | collective-permute-start | bytes 307208 | tf_op jit(solution)/shard_map/ppermute | solution.py:437
  51.0 2.9 %collective-permute-done.10 = bf16[1,400,128]{2,1,0:T(8,128)(2,1)S(1)} collective-permute-done((bf16[1,400,128]{2,1,0:T(8,128)(2,1)S(1)}, bf16[1,400,128]{2,1,0:T(8,128)(2,1)S(1)}, u32[]{:S(2)}, u32[]{:S(2)}) %collective-permute-start.10) | collective-permute-done | bytes 102432 | tf_op jit(solution)/shard_map/ppermute | solution.py:437
  53.9 3.3 %collective-permute-start.11 = (bf16[1,400,128]{2,1,0:T(8,128)(2,1)S(1)}, bf16[1,400,128]{2,1,0:T(8,128)(2,1)S(1)}, u32[]{:S(2)}, u32[]{:S(2)}) collective-permute-start(bf16[1,400,128]{2,1,0:T(8,128)(2,1)S(1)} %add_convert_fusion.3), channel_id=1, source_target_pairs={{0,16},{1,17},{2,18},{3,19},{4,20},{5,21},{6,22},{7,23},{8,24},{9,... | collective-permute-start | bytes 307208 | tf_op jit(solution)/shard_map/ppermute | solution.py:437
  57.3 3.7 %collective-permute-done.11 = bf16[1,400,128]{2,1,0:T(8,128)(2,1)S(1)} collective-permute-done((bf16[1,400,128]{2,1,0:T(8,128)(2,1)S(1)}, bf16[1,400,128]{2,1,0:T(8,128)(2,1)S(1)}, u32[]{:S(2)}, u32[]{:S(2)}) %collective-permute-start.11) | collective-permute-done | bytes 102432 | tf_op jit(solution)/shard_map/ppermute | solution.py:437
  67.4 3.0 %collective-permute-done.14 = bf16[1,400,128]{2,1,0:T(8,128)(2,1)S(1)} collective-permute-done((bf16[1,400,128]{2,1,0:T(8,128)(2,1)S(1)}, bf16[1,400,128]{2,1,0:T(8,128)(2,1)S(1)}, u32[]{:S(2)}, u32[]{:S(2)}) %collective-permute-start.14) | collective-permute-done | bytes 102432 | tf_op jit(solution)/shard_map/ppermute | solution.py:437
  70.5 2.5 %shard_map.118 = (bf16[2,32,640]{2,1,0:T(8,128)(2,1)S(1)}, f32[2,64,128]{2,1,0:T(8,128)S(1)}, f32[8,256]{1,0:T(8,128)S(1)}) custom-call(s32[38]{0:T(128)S(1)} %dynamic-slice_bitcast_fusion.slots, bf16[2,2,400,128]{3,2,1,0:T(8,128)(2,1)S(1)} %maximum_maximum_fusion.near, bf16[2,800,800]{2,1,0:T(8,128)(2,1)S(1)} %shard_map.113.pick, ...), custom_call_target="tpu_custom_call" | custom-call | tf_op jit(solution)/shard_map/pallas_call | solution.py:57
  73.1 3.0 %shard_map.119 = (f32[2,20,2,640]{3,2,1,0:T(2,128)S(1)}, f32[32,128]{1,0:T(8,128)S(1)}, f32[1,128]{1,0:T(1,128)S(1)}, f32[1,20,2,320]{3,2,1,0:T(2,128)S(1)}) custom-call(s32[38]{0:T(128)S(1)} %dynamic-slice_bitcast_fusion.slots, bf16[2,2,400,128]{3,2,1,0:T(8,128)(2,1)S(1)} %collective-permute-done.15.far, ...), custom_call_target="tpu_custom_call" | custom-call | tf_op jit(solution)/shard_map/pallas_call | solution.py:57
  76.1 13.1 %all_to_all.11 = f32[32,1,128]{2,1,0:T(1,128)S(1)} all-to-all(f32[32,1,128]{2,1,0:T(1,128)S(1)} %bitcast.41), channel_id=1, replica_groups=mesh['shot'=16,'coil'=2] {'shot','coil'}, dimensions={0} | all-to-all | bytes 32768 | tf_op jit(solution)/shard_map/all_to_all | solution.py:551
  (35 shorter events, 13.3 us)
Async XLA Ops:
  1.6 6.0 %collective-permute-start = (bf16[1,100,128]{2,1,0:T(8,128)(2,1)S(1)}, bf16[1,100,128]{2,1,0:T(8,128)(2,1)S(1)}, u32[]{:S(2)}, u32[]{:S(2)}) collective-permute-start(bf16[1,100,128]{2,1,0:T(8,128)(2,1)S(1)} %reshape.40), channel_id=1, source_target_pairs={{0,16},{1,17},{2,18},{3,19},{4,20},{5,21},{6,22},{7,23},{8,24},{9,... | collective-permute-start | bytes 76808 | tf_op jit(solution)/shard_map/ppermute | solution.py:437
  7.6 4.2 %collective-permute-start.1 = (bf16[2,100,128]{2,1,0:T(8,128)(2,1)S(1)}, bf16[2,100,128]{2,1,0:T(8,128)(2,1)S(1)}, u32[]{:S(2)}, u32[]{:S(2)}) collective-permute-start(bf16[2,100,128]{2,1,0:T(8,128)(2,1)S(1)} %pad_maximum_fusion), channel_id=1, source_target_pairs={{0,8},{1,9},{2,10},{3,11},{4,12},{5,13},{6,14},{7,15},{8,0},{9,1},... | collective-permute-start | bytes 153608 | tf_op jit(solution)/shard_map/ppermute | solution.py:437
  11.8 5.5 %collective-permute-start.2 = (bf16[4,100,128]{2,1,0:T(8,128)(2,1)S(1)}, bf16[4,100,128]{2,1,0:T(8,128)(2,1)S(1)}, u32[]{:S(2)}, u32[]{:S(2)}) collective-permute-start(bf16[4,100,128]{2,1,0:T(8,128)(2,1)S(1)} %get-tuple-element.46), channel_id=1, source_target_pairs={{0,4},{1,5},{2,3},{3,2},{4,0},{5,1},{6,7},{7,6},{8,12},{9,13},{10,... | collective-permute-start | bytes 307208 | tf_op jit(solution)/shard_map/ppermute | solution.py:437
  13.9 5.9 %collective-permute-start.3 = (bf16[4,100,128]{2,1,0:T(8,128)(2,1)S(1)}, bf16[4,100,128]{2,1,0:T(8,128)(2,1)S(1)}, u32[]{:S(2)}, u32[]{:S(2)}) collective-permute-start(bf16[4,100,128]{2,1,0:T(8,128)(2,1)S(1)} %get-tuple-element.46), channel_id=1, source_target_pairs={{0,1},{1,0},{2,6},{3,7},{4,5},{5,4},{6,2},{7,3},{8,9},{9,8},{10,14... | collective-permute-start | bytes 307208 | tf_op jit(solution)/shard_map/ppermute | solution.py:437
  17.3 5.0 %collective-permute-start.4 = (bf16[4,100,128]{2,1,0:T(8,128)(2,1)S(1)}, bf16[4,100,128]{2,1,0:T(8,128)(2,1)S(1)}, u32[]{:S(2)}, u32[]{:S(2)}) collective-permute-start(bf16[4,100,128]{2,1,0:T(8,128)(2,1)S(1)} %collective-permute-done.2), channel_id=1, source_target_pairs={{0,1},{1,0},{2,6},{3,7},{4,5},{5,4},{6,2},{7,3},{8,9},{9,8},{10,14... | collective-permute-start | bytes 307208 | tf_op jit(solution)/shard_map/ppermute | solution.py:437
  22.4 8.7 %collective-permute-start.5 = (bf16[16,100,128]{2,1,0:T(8,128)(2,1)S(1)}, bf16[16,100,128]{2,1,0:T(8,128)(2,1)S(1)}, u32[]{:S(2)}, u32[]{:S(2)}) collective-permute-start(bf16[16,100,128]{2,1,0:T(8,128)(2,1)S(1)} %constant_dynamic-update-slice_fusion.3.mine), channel_id=1, source_target_pairs={{0,2},{1,3},{2,0},{3,1},{4,6},{5,7},{6,4},{7,5},{8,10},{9,11},{10,... | collective-permute-start | bytes 1228808 | tf_op jit(solution)/shard_map/ppermute | solution.py:437
  37.2 2.2 %collective-permute-start.6 = (bf16[2,2,400,128]{3,2,1,0:T(8,128)(2,1)S(1)}, bf16[2,2,400,128]{3,2,1,0:T(8,128)(2,1)S(1)}, u32[]{:S(2)}, u32[]{:S(2)}) collective-permute-start(bf16[2,2,400,128]{3,2,1,0:T(8,128)(2,1)S(1)} %get-tuple-element.30), channel_id=1, source_target_pairs={{0,2},{1,3},{2,0},{3,1},{4,6},{5,7},{6,4},{7,5},{8,10},{9,11},{10,... | collective-permute-start | bytes 1228808 | tf_op jit(solution)/shard_map/ppermute | solution.py:437
  39.6 4.7 %collective-permute-start.8 = (bf16[1,400,128]{2,1,0:T(8,128)(2,1)S(1)}, bf16[1,400,128]{2,1,0:T(8,128)(2,1)S(1)}, u32[]{:S(2)}, u32[]{:S(2)}) collective-permute-start(bf16[1,400,128]{2,1,0:T(8,128)(2,1)S(1)} %get-tuple-element.45), channel_id=1, source_target_pairs={{0,1},{1,0},{2,6},{3,7},{4,5},{5,4},{6,2},{7,3},{8,9},{9,8},{10,14... | collective-permute-start | bytes 307208 | tf_op jit(solution)/shard_map/ppermute | solution.py:437
  41.7 4.7 %collective-permute-start.7 = (bf16[1,400,128]{2,1,0:T(8,128)(2,1)S(1)}, bf16[1,400,128]{2,1,0:T(8,128)(2,1)S(1)}, u32[]{:S(2)}, u32[]{:S(2)}) collective-permute-start(bf16[1,400,128]{2,1,0:T(8,128)(2,1)S(1)} %get-tuple-element.44), channel_id=1, source_target_pairs={{0,1},{1,0},{2,6},{3,7},{4,5},{5,4},{6,2},{7,3},{8,9},{9,8},{10,14... | collective-permute-start | bytes 307208 | tf_op jit(solution)/shard_map/ppermute | solution.py:437
  44.4 4.7 %collective-permute-start.9 = (bf16[1,400,128]{2,1,0:T(8,128)(2,1)S(1)}, bf16[1,400,128]{2,1,0:T(8,128)(2,1)S(1)}, u32[]{:S(2)}, u32[]{:S(2)}) collective-permute-start(bf16[1,400,128]{2,1,0:T(8,128)(2,1)S(1)} %fusion), channel_id=1, source_target_pairs={{0,4},{1,5},{2,3},{3,2},{4,0},{5,1},{6,7},{7,6},{8,12},{9,13},{10,... | collective-permute-start | bytes 307208 | tf_op jit(solution)/shard_map/ppermute | solution.py:437
  49.2 4.7 %collective-permute-start.10 = (bf16[1,400,128]{2,1,0:T(8,128)(2,1)S(1)}, bf16[1,400,128]{2,1,0:T(8,128)(2,1)S(1)}, u32[]{:S(2)}, u32[]{:S(2)}) collective-permute-start(bf16[1,400,128]{2,1,0:T(8,128)(2,1)S(1)} %add_convert_fusion.4), channel_id=1, source_target_pairs={{0,8},{1,9},{2,10},{3,11},{4,12},{5,13},{6,14},{7,15},{8,0},{9,1},... | collective-permute-start | bytes 307208 | tf_op jit(solution)/shard_map/ppermute | solution.py:437
  53.9 7.1 %collective-permute-start.11 = (bf16[1,400,128]{2,1,0:T(8,128)(2,1)S(1)}, bf16[1,400,128]{2,1,0:T(8,128)(2,1)S(1)}, u32[]{:S(2)}, u32[]{:S(2)}) collective-permute-start(bf16[1,400,128]{2,1,0:T(8,128)(2,1)S(1)} %add_convert_fusion.3), channel_id=1, source_target_pairs={{0,16},{1,17},{2,18},{3,19},{4,20},{5,21},{6,22},{7,23},{8,24},{9,... | collective-permute-start | bytes 307208 | tf_op jit(solution)/shard_map/ppermute | solution.py:437
  61.0 4.7 %collective-permute-start.12 = (bf16[1,400,128]{2,1,0:T(8,128)(2,1)S(1)}, bf16[1,400,128]{2,1,0:T(8,128)(2,1)S(1)}, u32[]{:S(2)}, u32[]{:S(2)}) collective-permute-start(bf16[1,400,128]{2,1,0:T(8,128)(2,1)S(1)} %add_convert_fusion.2), channel_id=1, source_target_pairs={{0,4},{1,5},{2,3},{3,2},{4,0},{5,1},{6,7},{7,6},{8,12},{9,13},{10,... | collective-permute-start | bytes 307208 | tf_op jit(solution)/shard_map/ppermute | solution.py:437
  62.7 4.7 %collective-permute-start.13 = (bf16[1,400,128]{2,1,0:T(8,128)(2,1)S(1)}, bf16[1,400,128]{2,1,0:T(8,128)(2,1)S(1)}, u32[]{:S(2)}, u32[]{:S(2)}) collective-permute-start(bf16[1,400,128]{2,1,0:T(8,128)(2,1)S(1)} %add_convert_fusion.2), channel_id=1, source_target_pairs={{0,1},{1,0},{2,6},{3,7},{4,5},{5,4},{6,2},{7,3},{8,9},{9,8},{10,14... | collective-permute-start | bytes 307208 | tf_op jit(solution)/shard_map/ppermute | solution.py:437
  65.7 4.7 %collective-permute-start.14 = (bf16[1,400,128]{2,1,0:T(8,128)(2,1)S(1)}, bf16[1,400,128]{2,1,0:T(8,128)(2,1)S(1)}, u32[]{:S(2)}, u32[]{:S(2)}) collective-permute-start(bf16[1,400,128]{2,1,0:T(8,128)(2,1)S(1)} %collective-permute-done.12), channel_id=1, source_target_pairs={{0,1},{1,0},{2,6},{3,7},{4,5},{5,4},{6,2},{7,3},{8,9},{9,8},{10,14... | collective-permute-start | bytes 307208 | tf_op jit(solution)/shard_map/ppermute | solution.py:437
  70.5 2.6 %collective-permute-start.15 = (bf16[2,2,400,128]{3,2,1,0:T(8,128)(2,1)S(1)}, bf16[2,2,400,128]{3,2,1,0:T(8,128)(2,1)S(1)}, u32[]{:S(2)}, u32[]{:S(2)}) collective-permute-start(bf16[2,2,400,128]{3,2,1,0:T(8,128)(2,1)S(1)} %maximum_maximum_fusion.near), channel_id=1, source_target_pairs={{0,2},{1,3},{2,0},{3,1},{4,6},{5,7},{6,4},{7,5},{8,10},{9,11},{10,... | collective-permute-start | bytes 1228808 | tf_op jit(solution)/shard_map/ppermute | solution.py:437
where the time goes:
time: 90.5 us; the launch traced here: 90.1 us
  starting transfers between devices  27 us (30%)
  waiting for transfers between devices  25 us (28%)
  Pallas kernels  22.1 us (24%)
  blocking collectives  13.1 us (14%)
  other arithmetic  1.15 us (1%)
  local copies, waits for them, and re-layouts  0.91 us (1%)
    ppermute x16, starting transfers between devices, swap(): return lax.ppermute(value, AXES, exchange_pairs(partner, shots, coil_parts))  27 us
    ppermute x16, waiting for transfers between devices, swap(): return lax.ppermute(value, AXES, exchange_pairs(partner, shots, coil_parts))  25 us
    pallas_call x8, Pallas kernels, run(): pl.pallas_call(body, out_shape=out_shape, in_specs=specs, out_specs=jax.t...  22.1 us
    all_to_all x1, blocking collectives, shards(): totals = lax.all_to_all(sums, AXES, 0, 0, tiled=True)  13.1 us
  transfers between devices with their start and end apart: 16, of which 10 were waited for; matrix products, arithmetic and copies ran while one was open for 1% of the time, Pallas kernels for 13%

commit v1 on v0

--- a/solution.py
+++ b/solution.py
@@ -75,28 +75,22 @@
     return copies
 
 
-def wanted_of(source_far, live_far, source, live, sems):
+def spread_body(wanted, spread):
+    down = lax.broadcasted_iota(jnp.int32, spread.shape, 0)
+    spread[...] = jnp.where(down == jnp.broadcast_to(wanted[...], spread.shape), 1.0, 0.0).astype(BF)
+
+
+def pick_body(slots, source_far, live_far, pick, wanted, source, live, sems):
+    members, blocks, _ = pick.shape
     for copy in fetch([(source_far, source), (live_far, live)], sems):
         copy.wait()
-    return jnp.where(live[...] != 0, source[...], -1)
-
-
-def spread_body(slots, source_far, live_far, spread, source, live, wanted, sems):
-    blocks, wide = spread.shape
-    table = wanted_of(source_far, live_far, source, live, sems)
-    for k in range(wide // blocks):
-        wanted[:, k * blocks : (k + 1) * blocks] = table[k : k + 1, :]
-    down = lax.broadcasted_iota(jnp.int32, (blocks, wide), 0)
-    spread[...] = jnp.where(down == jnp.broadcast_to(wanted[...], (blocks, wide)), 1.0, 0.0).astype(BF)
-
-
-def pick_body(slots, source_far, live_far, pick, source, live, sems):
-    members, blocks, _ = pick.shape
-    table = wanted_of(source_far, live_far, source, live, sems)
+    table = jnp.where(live[...] != 0, source[...], -1)
     full = round_up(blocks, 128)
     along = lax.broadcasted_iota(jnp.int32, (blocks, blocks), 1).astype(F32)
     for k in range(members):
-        flat = jnp.broadcast_to(table[k : k + 1, :], (8, blocks)).astype(F32)
+        by_col = table[k : k + 1, :]
+        wanted[:, k * blocks : (k + 1) * blocks] = by_col
+        flat = jnp.broadcast_to(by_col, (8, blocks)).astype(F32)
         if full > blocks:
             flat = jnp.concatenate([flat, jnp.zeros((8, full - blocks), F32)], axis=1)
         by_row = flat.T[:blocks, :1]
@@ -456,15 +450,15 @@
     shape = jax.ShapeDtypeStruct
     vmem = lambda value: pltpu.VMEM(value.shape, value.dtype)
     source, live = warp_source[0].T, warp_live[0].T
-    both = [vmem(source), vmem(live)]
-    sems = pltpu.SemaphoreType.DMA((2,))
-    spread = call(
-        spread_body, shape((blocks, members * blocks), BF), slices,
-        scratch=both + [pltpu.VMEM((1, members * blocks), jnp.int32), sems], smem=1, far=2,
+    pick, wanted = call(
+        pick_body,
+        [shape((members, blocks, blocks), BF), shape((1, members * blocks), jnp.int32)],
+        slices,
+        scratch=[vmem(source), vmem(live), pltpu.SemaphoreType.DMA((2,))],
+        smem=1,
+        far=2,
     )(slots, source, live)
-    pick = call(
-        pick_body, shape((members, blocks, blocks), BF), slices, scratch=both + [sems], smem=1, far=2,
-    )(slots, source, live)
+    spread = call(spread_body, shape((blocks, members * blocks), BF), slices)(wanted)
     seen = measured[0].transpose(0, 2, 1, 3)
     rows_first = image.transpose(0, 2, 1, 3)
     kept = [readout, kernels, seen, rows_first]
@@ -511,7 +505,7 @@
     out3, total = add(stay2[:, 1], got), add(stay2[:, 0], stay_got)
     got = swap(out3, second_way)
     total = add(total, got)
-    for partner in rest:
+    for partner in reversed(rest):
         total = add(total, swap(total, partner))
     second = swap(total, second_way)
     early = swap(total, first_way)

time: 90.5 us -> 88.2 us (0.975)
  Pallas kernels: 22.1 us -> 20.1 us
  waiting for transfers between devices: 25 us -> 23.2 us
  starting transfers between devices: 27 us -> 28.6 us
    pallas_call x8, Pallas kernels: 22.1 us -> 20.1 us  [run(): pl.pallas_call(body, out_shape=out_shape, in_specs=specs, out_specs=jax.t...]
    ppermute x16, waiting for transfers between devices: 25 us -> 23.2 us  [swap(): return lax.ppermute(value, AXES, exchange_pairs(partner, shots, coil_parts))]
    ppermute x16, starting transfers between devices: 27 us -> 28.6 us  [swap(): return lax.ppermute(value, AXES, exchange_pairs(partner, shots, coil_parts))]
  transfers between devices with their start and end apart: 16 -> 16, of which waited for: 10 -> 10; matrix products, arithmetic and copies ran while one was open for 1% -> 1% of each run, Pallas kernels for 13% -> 11%
where the time goes in v1:
time: 88.2 us; the launch traced here: 87.8 us
  starting transfers between devices  28.6 us (32%)
  waiting for transfers between devices  23.2 us (26%)
  Pallas kernels  20.1 us (23%)
  blocking collectives  13.1 us (15%)
  other arithmetic  1.15 us (1%)
  local copies, waits for them, and re-layouts  0.91 us (1%)
    ppermute x16, starting transfers between devices, swap(): return lax.ppermute(value, AXES, exchange_pairs(partner, shots, coil_parts))  28.6 us
    ppermute x16, waiting for transfers between devices, swap(): return lax.ppermute(value, AXES, exchange_pairs(partner, shots, coil_parts))  23.2 us
    pallas_call x8, Pallas kernels, run(): pl.pallas_call(body, out_shape=out_shape, in_specs=specs, out_specs=jax.t...  20.1 us
    all_to_all x1, blocking collectives, shards(): totals = lax.all_to_all(sums, AXES, 0, 0, tiled=True)  13.1 us
  transfers between devices with their start and end apart: 16, of which 10 were waited for; matrix products, arithmetic and copies ran while one was open for 1% of the time, Pallas kernels for 11%

profile of v1, /device:TPU:0, one launch (start us, length us, event | category | flops | bytes accessed | tf_op | source)
XLA Modules:
  0.0 87.8 jit_solution(17530703929870120453)
XLA Ops:
  1.6 4.1 %collective-permute-start = (bf16[1,100,128]{2,1,0:T(8,128)(2,1)S(1)}, bf16[1,100,128]{2,1,0:T(8,128)(2,1)S(1)}, u32[]{:S(2)}, u32[]{:S(2)}) collective-permute-start(bf16[1,100,128]{2,1,0:T(8,128)(2,1)S(1)} %reshape.40), channel_id=1, source_target_pairs={{0,16},{1,17},{2,18},{3,19},{4,20},{5,21},{6,22},{7,23},{8,24},{9,... | collective-permute-start | bytes 76808 | tf_op jit(solution)/shard_map/ppermute | solution.py:431
  7.6 2.0 %collective-permute-start.1 = (bf16[2,100,128]{2,1,0:T(8,128)(2,1)S(1)}, bf16[2,100,128]{2,1,0:T(8,128)(2,1)S(1)}, u32[]{:S(2)}, u32[]{:S(2)}) collective-permute-start(bf16[2,100,128]{2,1,0:T(8,128)(2,1)S(1)} %pad_maximum_fusion), channel_id=1, source_target_pairs={{0,8},{1,9},{2,10},{3,11},{4,12},{5,13},{6,14},{7,15},{8,0},{9,1},... | collective-permute-start | bytes 153608 | tf_op jit(solution)/shard_map/ppermute | solution.py:431
  9.6 2.2 %collective-permute-done.1 = bf16[2,100,128]{2,1,0:T(8,128)(2,1)S(1)} collective-permute-done((bf16[2,100,128]{2,1,0:T(8,128)(2,1)S(1)}, bf16[2,100,128]{2,1,0:T(8,128)(2,1)S(1)}, u32[]{:S(2)}, u32[]{:S(2)}) %collective-permute-start.1) | collective-permute-done | bytes 51232 | tf_op jit(solution)/shard_map/ppermute | solution.py:431
  11.8 2.0 %collective-permute-start.2 = (bf16[4,100,128]{2,1,0:T(8,128)(2,1)S(1)}, bf16[4,100,128]{2,1,0:T(8,128)(2,1)S(1)}, u32[]{:S(2)}, u32[]{:S(2)}) collective-permute-start(bf16[4,100,128]{2,1,0:T(8,128)(2,1)S(1)} %get-tuple-element.50), channel_id=1, source_target_pairs={{0,4},{1,5},{2,3},{3,2},{4,0},{5,1},{6,7},{7,6},{8,12},{9,13},{10,... | collective-permute-start | bytes 307208 | tf_op jit(solution)/shard_map/ppermute | solution.py:431
  15.4 2.0 %collective-permute-done.2 = bf16[4,100,128]{2,1,0:T(8,128)(2,1)S(1)} collective-permute-done((bf16[4,100,128]{2,1,0:T(8,128)(2,1)S(1)}, bf16[4,100,128]{2,1,0:T(8,128)(2,1)S(1)}, u32[]{:S(2)}, u32[]{:S(2)}) %collective-permute-start.2) | collective-permute-done | bytes 102432 | tf_op jit(solution)/shard_map/ppermute | solution.py:431
  17.3 2.4 %collective-permute-start.4 = (bf16[4,100,128]{2,1,0:T(8,128)(2,1)S(1)}, bf16[4,100,128]{2,1,0:T(8,128)(2,1)S(1)}, u32[]{:S(2)}, u32[]{:S(2)}) collective-permute-start(bf16[4,100,128]{2,1,0:T(8,128)(2,1)S(1)} %collective-permute-done.2), channel_id=1, source_target_pairs={{0,1},{1,0},{2,6},{3,7},{4,5},{5,4},{6,2},{7,3},{8,9},{9,8},{10,14... | collective-permute-start | bytes 307208 | tf_op jit(solution)/shard_map/ppermute | solution.py:431
  19.7 2.6 %collective-permute-done.4 = bf16[4,100,128]{2,1,0:T(8,128)(2,1)S(1)} collective-permute-done((bf16[4,100,128]{2,1,0:T(8,128)(2,1)S(1)}, bf16[4,100,128]{2,1,0:T(8,128)(2,1)S(1)}, u32[]{:S(2)}, u32[]{:S(2)}) %collective-permute-start.4) | collective-permute-done | bytes 102432 | tf_op jit(solution)/shard_map/ppermute | solution.py:431
  23.2 2.1 %shard_map.113 = (bf16[2,800,800]{2,1,0:T(8,128)(2,1)S(1)}, s32[1,1600]{1,0:T(1,128)S(1)}) custom-call(s32[38]{0:T(128)S(1)} %dynamic-slice_bitcast_fusion.slots, s32[2,800]{1,0:T(2,128)} %bitcast.50, s32[2,800]{1,0:T(2,128)} %bitcast.51), custom_call_target="tpu_custom_call" | custom-call | tf_op jit(solution)/shard_map/pallas_call | solution.py:57
  25.7 3.3 %shard_map.115 = (bf16[128,320]{1,0:T(8,128)(2,1)S(1)}, bf16[320,128]{1,0:T(8,128)(2,1)S(1)}, bf16[4,160,640]{2,1,0:T(8,128)(2,1)S(1)}, bf16[4,160,640]{2,1,0:T(...) custom-call(bf16[2,4,320,320]{3,2,1,0:T(8,128)(2,1)} %bitcast.42, ...), custom_call_target="tpu_custom_call" | custom-call | tf_op jit(solution)/shard_map/pallas_call | solution.py:57
  29.0 6.2 %shard_map.116 = (f32[2,20,2,640]{3,2,1,0:T(2,128)S(1)}, bf16[2,2,400,128]{3,2,1,0:T(8,128)(2,1)S(1)}, bf16[2,800,128]{2,1,0:T(8,128)(2,1)S(1)}) custom-call(s32[38]{0:T(128)S(1)} %dynamic-slice_bitcast_fusion.slots, bf16[16,100,128]{2,1,0:T(8,128)(2,1)S(1)} %constant_dynamic-update-slice_fusion.3.mine, ...), custom_call_target="tpu_custom_call" | custom-call | tf_op jit(solution)/shard_map/pallas_call | solution.py:57
  37.6 2.1 %collective-permute-start.8 = (bf16[1,400,128]{2,1,0:T(8,128)(2,1)S(1)}, bf16[1,400,128]{2,1,0:T(8,128)(2,1)S(1)}, u32[]{:S(2)}, u32[]{:S(2)}) collective-permute-start(bf16[1,400,128]{2,1,0:T(8,128)(2,1)S(1)} %get-tuple-element.49), channel_id=1, source_target_pairs={{0,1},{1,0},{2,6},{3,7},{4,5},{5,4},{6,2},{7,3},{8,9},{9,8},{10,14... | collective-permute-start | bytes 307208 | tf_op jit(solution)/shard_map/ppermute | solution.py:431
  39.7 2.6 %collective-permute-done.8 = bf16[1,400,128]{2,1,0:T(8,128)(2,1)S(1)} collective-permute-done((bf16[1,400,128]{2,1,0:T(8,128)(2,1)S(1)}, bf16[1,400,128]{2,1,0:T(8,128)(2,1)S(1)}, u32[]{:S(2)}, u32[]{:S(2)}) %collective-permute-start.8) | collective-permute-done | bytes 102432 | tf_op jit(solution)/shard_map/ppermute | solution.py:431
  42.3 2.0 %collective-permute-start.9 = (bf16[1,400,128]{2,1,0:T(8,128)(2,1)S(1)}, bf16[1,400,128]{2,1,0:T(8,128)(2,1)S(1)}, u32[]{:S(2)}, u32[]{:S(2)}) collective-permute-start(bf16[1,400,128]{2,1,0:T(8,128)(2,1)S(1)} %fusion), channel_id=1, source_target_pairs={{0,4},{1,5},{2,3},{3,2},{4,0},{5,1},{6,7},{7,6},{8,12},{9,13},{10,... | collective-permute-start | bytes 307208 | tf_op jit(solution)/shard_map/ppermute | solution.py:431
  44.4 2.7 %collective-permute-done.9 = bf16[1,400,128]{2,1,0:T(8,128)(2,1)S(1)} collective-permute-done((bf16[1,400,128]{2,1,0:T(8,128)(2,1)S(1)}, bf16[1,400,128]{2,1,0:T(8,128)(2,1)S(1)}, u32[]{:S(2)}, u32[]{:S(2)}) %collective-permute-start.9) | collective-permute-done | bytes 102432 | tf_op jit(solution)/shard_map/ppermute | solution.py:431
  47.1 2.9 %collective-permute-start.10 = (bf16[1,400,128]{2,1,0:T(8,128)(2,1)S(1)}, bf16[1,400,128]{2,1,0:T(8,128)(2,1)S(1)}, u32[]{:S(2)}, u32[]{:S(2)}) collective-permute-start(bf16[1,400,128]{2,1,0:T(8,128)(2,1)S(1)} %add_convert_fusion.4), channel_id=1, source_target_pairs={{0,16},{1,17},{2,18},{3,19},{4,20},{5,21},{6,22},{7,23},{8,24},{9,... | collective-permute-start | bytes 307208 | tf_op jit(solution)/shard_map/ppermute | solution.py:431
  50.0 2.7 %collective-permute-done.10 = bf16[1,400,128]{2,1,0:T(8,128)(2,1)S(1)} collective-permute-done((bf16[1,400,128]{2,1,0:T(8,128)(2,1)S(1)}, bf16[1,400,128]{2,1,0:T(8,128)(2,1)S(1)}, u32[]{:S(2)}, u32[]{:S(2)}) %collective-permute-start.10) | collective-permute-done | bytes 102432 | tf_op jit(solution)/shard_map/ppermute | solution.py:431
  52.8 2.1 %collective-permute-start.11 = (bf16[1,400,128]{2,1,0:T(8,128)(2,1)S(1)}, bf16[1,400,128]{2,1,0:T(8,128)(2,1)S(1)}, u32[]{:S(2)}, u32[]{:S(2)}) collective-permute-start(bf16[1,400,128]{2,1,0:T(8,128)(2,1)S(1)} %add_convert_fusion.3), channel_id=1, source_target_pairs={{0,8},{1,9},{2,10},{3,11},{4,12},{5,13},{6,14},{7,15},{8,0},{9,1},... | collective-permute-start | bytes 307208 | tf_op jit(solution)/shard_map/ppermute | solution.py:431
  54.9 2.6 %collective-permute-done.11 = bf16[1,400,128]{2,1,0:T(8,128)(2,1)S(1)} collective-permute-done((bf16[1,400,128]{2,1,0:T(8,128)(2,1)S(1)}, bf16[1,400,128]{2,1,0:T(8,128)(2,1)S(1)}, u32[]{:S(2)}, u32[]{:S(2)}) %collective-permute-start.11) | collective-permute-done | bytes 102432 | tf_op jit(solution)/shard_map/ppermute | solution.py:431
  57.6 3.2 %collective-permute-start.12 = (bf16[1,400,128]{2,1,0:T(8,128)(2,1)S(1)}, bf16[1,400,128]{2,1,0:T(8,128)(2,1)S(1)}, u32[]{:S(2)}, u32[]{:S(2)}) collective-permute-start(bf16[1,400,128]{2,1,0:T(8,128)(2,1)S(1)} %add_convert_fusion.2), channel_id=1, source_target_pairs={{0,4},{1,5},{2,3},{3,2},{4,0},{5,1},{6,7},{7,6},{8,12},{9,13},{10,... | collective-permute-start | bytes 307208 | tf_op jit(solution)/shard_map/ppermute | solution.py:431
  63.5 1.9 %collective-permute-start.14 = (bf16[1,400,128]{2,1,0:T(8,128)(2,1)S(1)}, bf16[1,400,128]{2,1,0:T(8,128)(2,1)S(1)}, u32[]{:S(2)}, u32[]{:S(2)}) collective-permute-start(bf16[1,400,128]{2,1,0:T(8,128)(2,1)S(1)} %collective-permute-done.12), channel_id=1, source_target_pairs={{0,1},{1,0},{2,6},{3,7},{4,5},{5,4},{6,2},{7,3},{8,9},{9,8},{10,14... | collective-permute-start | bytes 307208 | tf_op jit(solution)/shard_map/ppermute | solution.py:431
  65.5 2.7 %collective-permute-done.14 = bf16[1,400,128]{2,1,0:T(8,128)(2,1)S(1)} collective-permute-done((bf16[1,400,128]{2,1,0:T(8,128)(2,1)S(1)}, bf16[1,400,128]{2,1,0:T(8,128)(2,1)S(1)}, u32[]{:S(2)}, u32[]{:S(2)}) %collective-permute-start.14) | collective-permute-done | bytes 102432 | tf_op jit(solution)/shard_map/ppermute | solution.py:431
  68.3 2.5 %shard_map.118 = (bf16[2,32,640]{2,1,0:T(8,128)(2,1)S(1)}, f32[2,64,128]{2,1,0:T(8,128)S(1)}, f32[8,256]{1,0:T(8,128)S(1)}) custom-call(s32[38]{0:T(128)S(1)} %dynamic-slice_bitcast_fusion.slots, bf16[2,2,400,128]{3,2,1,0:T(8,128)(2,1)S(1)} %maximum_maximum_fusion.near, bf16[2,800,800]{2,1,0:T(8,128)(2,1)S(1)} %get-tuple-element.24.pick, ...), custom_call_target="tpu_custom_call" | custom-call | tf_op jit(solution)/shard_map/pallas_call | solution.py:57
  70.9 3.0 %shard_map.119 = (f32[2,20,2,640]{3,2,1,0:T(2,128)S(1)}, f32[32,128]{1,0:T(8,128)S(1)}, f32[1,128]{1,0:T(1,128)S(1)}, f32[1,20,2,320]{3,2,1,0:T(2,128)S(1)}) custom-call(s32[38]{0:T(128)S(1)} %dynamic-slice_bitcast_fusion.slots, bf16[2,2,400,128]{3,2,1,0:T(8,128)(2,1)S(1)} %collective-permute-done.15.far, ...), custom_call_target="tpu_custom_call" | custom-call | tf_op jit(solution)/shard_map/pallas_call | solution.py:57
  73.9 13.1 %all_to_all.11 = f32[32,1,128]{2,1,0:T(1,128)S(1)} all-to-all(f32[32,1,128]{2,1,0:T(1,128)S(1)} %bitcast.41), channel_id=1, replica_groups=mesh['shot'=16,'coil'=2] {'shot','coil'}, dimensions={0} | all-to-all | bytes 32768 | tf_op jit(solution)/shard_map/all_to_all | solution.py:545
  (35 shorter events, 12.0 us)
Async XLA Ops:
  1.6 6.0 %collective-permute-start = (bf16[1,100,128]{2,1,0:T(8,128)(2,1)S(1)}, bf16[1,100,128]{2,1,0:T(8,128)(2,1)S(1)}, u32[]{:S(2)}, u32[]{:S(2)}) collective-permute-start(bf16[1,100,128]{2,1,0:T(8,128)(2,1)S(1)} %reshape.40), channel_id=1, source_target_pairs={{0,16},{1,17},{2,18},{3,19},{4,20},{5,21},{6,22},{7,23},{8,24},{9,... | collective-permute-start | bytes 76808 | tf_op jit(solution)/shard_map/ppermute | solution.py:431
  7.6 4.2 %collective-permute-start.1 = (bf16[2,100,128]{2,1,0:T(8,128)(2,1)S(1)}, bf16[2,100,128]{2,1,0:T(8,128)(2,1)S(1)}, u32[]{:S(2)}, u32[]{:S(2)}) collective-permute-start(bf16[2,100,128]{2,1,0:T(8,128)(2,1)S(1)} %pad_maximum_fusion), channel_id=1, source_target_pairs={{0,8},{1,9},{2,10},{3,11},{4,12},{5,13},{6,14},{7,15},{8,0},{9,1},... | collective-permute-start | bytes 153608 | tf_op jit(solution)/shard_map/ppermute | solution.py:431
  11.8 5.5 %collective-permute-start.2 = (bf16[4,100,128]{2,1,0:T(8,128)(2,1)S(1)}, bf16[4,100,128]{2,1,0:T(8,128)(2,1)S(1)}, u32[]{:S(2)}, u32[]{:S(2)}) collective-permute-start(bf16[4,100,128]{2,1,0:T(8,128)(2,1)S(1)} %get-tuple-element.50), channel_id=1, source_target_pairs={{0,4},{1,5},{2,3},{3,2},{4,0},{5,1},{6,7},{7,6},{8,12},{9,13},{10,... | collective-permute-start | bytes 307208 | tf_op jit(solution)/shard_map/ppermute | solution.py:431
  13.9 5.9 %collective-permute-start.3 = (bf16[4,100,128]{2,1,0:T(8,128)(2,1)S(1)}, bf16[4,100,128]{2,1,0:T(8,128)(2,1)S(1)}, u32[]{:S(2)}, u32[]{:S(2)}) collective-permute-start(bf16[4,100,128]{2,1,0:T(8,128)(2,1)S(1)} %get-tuple-element.50), channel_id=1, source_target_pairs={{0,1},{1,0},{2,6},{3,7},{4,5},{5,4},{6,2},{7,3},{8,9},{9,8},{10,14... | collective-permute-start | bytes 307208 | tf_op jit(solution)/shard_map/ppermute | solution.py:431
  17.3 5.0 %collective-permute-start.4 = (bf16[4,100,128]{2,1,0:T(8,128)(2,1)S(1)}, bf16[4,100,128]{2,1,0:T(8,128)(2,1)S(1)}, u32[]{:S(2)}, u32[]{:S(2)}) collective-permute-start(bf16[4,100,128]{2,1,0:T(8,128)(2,1)S(1)} %collective-permute-done.2), channel_id=1, source_target_pairs={{0,1},{1,0},{2,6},{3,7},{4,5},{5,4},{6,2},{7,3},{8,9},{9,8},{10,14... | collective-permute-start | bytes 307208 | tf_op jit(solution)/shard_map/ppermute | solution.py:431
  22.4 6.6 %collective-permute-start.5 = (bf16[16,100,128]{2,1,0:T(8,128)(2,1)S(1)}, bf16[16,100,128]{2,1,0:T(8,128)(2,1)S(1)}, u32[]{:S(2)}, u32[]{:S(2)}) collective-permute-start(bf16[16,100,128]{2,1,0:T(8,128)(2,1)S(1)} %constant_dynamic-update-slice_fusion.3.mine), channel_id=1, source_target_pairs={{0,2},{1,3},{2,0},{3,1},{4,6},{5,7},{6,4},{7,5},{8,10},{9,11},{10,... | collective-permute-start | bytes 1228808 | tf_op jit(solution)/shard_map/ppermute | solution.py:431
  35.2 2.2 %collective-permute-start.6 = (bf16[2,2,400,128]{3,2,1,0:T(8,128)(2,1)S(1)}, bf16[2,2,400,128]{3,2,1,0:T(8,128)(2,1)S(1)}, u32[]{:S(2)}, u32[]{:S(2)}) collective-permute-start(bf16[2,2,400,128]{3,2,1,0:T(8,128)(2,1)S(1)} %get-tuple-element.34), channel_id=1, source_target_pairs={{0,2},{1,3},{2,0},{3,1},{4,6},{5,7},{6,4},{7,5},{8,10},{9,11},{10,... | collective-permute-start | bytes 1228808 | tf_op jit(solution)/shard_map/ppermute | solution.py:431
  37.6 4.7 %collective-permute-start.8 = (bf16[1,400,128]{2,1,0:T(8,128)(2,1)S(1)}, bf16[1,400,128]{2,1,0:T(8,128)(2,1)S(1)}, u32[]{:S(2)}, u32[]{:S(2)}) collective-permute-start(bf16[1,400,128]{2,1,0:T(8,128)(2,1)S(1)} %get-tuple-element.49), channel_id=1, source_target_pairs={{0,1},{1,0},{2,6},{3,7},{4,5},{5,4},{6,2},{7,3},{8,9},{9,8},{10,14... | collective-permute-start | bytes 307208 | tf_op jit(solution)/shard_map/ppermute | solution.py:431
  39.7 4.7 %collective-permute-start.7 = (bf16[1,400,128]{2,1,0:T(8,128)(2,1)S(1)}, bf16[1,400,128]{2,1,0:T(8,128)(2,1)S(1)}, u32[]{:S(2)}, u32[]{:S(2)}) collective-permute-start(bf16[1,400,128]{2,1,0:T(8,128)(2,1)S(1)} %get-tuple-element.48), channel_id=1, source_target_pairs={{0,1},{1,0},{2,6},{3,7},{4,5},{5,4},{6,2},{7,3},{8,9},{9,8},{10,14... | collective-permute-start | bytes 307208 | tf_op jit(solution)/shard_map/ppermute | solution.py:431
  42.3 4.7 %collective-permute-start.9 = (bf16[1,400,128]{2,1,0:T(8,128)(2,1)S(1)}, bf16[1,400,128]{2,1,0:T(8,128)(2,1)S(1)}, u32[]{:S(2)}, u32[]{:S(2)}) collective-permute-start(bf16[1,400,128]{2,1,0:T(8,128)(2,1)S(1)} %fusion), channel_id=1, source_target_pairs={{0,4},{1,5},{2,3},{3,2},{4,0},{5,1},{6,7},{7,6},{8,12},{9,13},{10,... | collective-permute-start | bytes 307208 | tf_op jit(solution)/shard_map/ppermute | solution.py:431
  47.1 5.6 %collective-permute-start.10 = (bf16[1,400,128]{2,1,0:T(8,128)(2,1)S(1)}, bf16[1,400,128]{2,1,0:T(8,128)(2,1)S(1)}, u32[]{:S(2)}, u32[]{:S(2)}) collective-permute-start(bf16[1,400,128]{2,1,0:T(8,128)(2,1)S(1)} %add_convert_fusion.4), channel_id=1, source_target_pairs={{0,16},{1,17},{2,18},{3,19},{4,20},{5,21},{6,22},{7,23},{8,24},{9,... | collective-permute-start | bytes 307208 | tf_op jit(solution)/shard_map/ppermute | solution.py:431
  52.8 4.7 %collective-permute-start.11 = (bf16[1,400,128]{2,1,0:T(8,128)(2,1)S(1)}, bf16[1,400,128]{2,1,0:T(8,128)(2,1)S(1)}, u32[]{:S(2)}, u32[]{:S(2)}) collective-permute-start(bf16[1,400,128]{2,1,0:T(8,128)(2,1)S(1)} %add_convert_fusion.3), channel_id=1, source_target_pairs={{0,8},{1,9},{2,10},{3,11},{4,12},{5,13},{6,14},{7,15},{8,0},{9,1},... | collective-permute-start | bytes 307208 | tf_op jit(solution)/shard_map/ppermute | solution.py:431
  57.6 6.0 %collective-permute-start.12 = (bf16[1,400,128]{2,1,0:T(8,128)(2,1)S(1)}, bf16[1,400,128]{2,1,0:T(8,128)(2,1)S(1)}, u32[]{:S(2)}, u32[]{:S(2)}) collective-permute-start(bf16[1,400,128]{2,1,0:T(8,128)(2,1)S(1)} %add_convert_fusion.2), channel_id=1, source_target_pairs={{0,4},{1,5},{2,3},{3,2},{4,0},{5,1},{6,7},{7,6},{8,12},{9,13},{10,... | collective-permute-start | bytes 307208 | tf_op jit(solution)/shard_map/ppermute | solution.py:431
  60.8 4.7 %collective-permute-start.13 = (bf16[1,400,128]{2,1,0:T(8,128)(2,1)S(1)}, bf16[1,400,128]{2,1,0:T(8,128)(2,1)S(1)}, u32[]{:S(2)}, u32[]{:S(2)}) collective-permute-start(bf16[1,400,128]{2,1,0:T(8,128)(2,1)S(1)} %add_convert_fusion.2), channel_id=1, source_target_pairs={{0,1},{1,0},{2,6},{3,7},{4,5},{5,4},{6,2},{7,3},{8,9},{9,8},{10,14... | collective-permute-start | bytes 307208 | tf_op jit(solution)/shard_map/ppermute | solution.py:431
  63.5 4.7 %collective-permute-start.14 = (bf16[1,400,128]{2,1,0:T(8,128)(2,1)S(1)}, bf16[1,400,128]{2,1,0:T(8,128)(2,1)S(1)}, u32[]{:S(2)}, u32[]{:S(2)}) collective-permute-start(bf16[1,400,128]{2,1,0:T(8,128)(2,1)S(1)} %collective-permute-done.12), channel_id=1, source_target_pairs={{0,1},{1,0},{2,6},{3,7},{4,5},{5,4},{6,2},{7,3},{8,9},{9,8},{10,14... | collective-permute-start | bytes 307208 | tf_op jit(solution)/shard_map/ppermute | solution.py:431
  68.2 2.6 %collective-permute-start.15 = (bf16[2,2,400,128]{3,2,1,0:T(8,128)(2,1)S(1)}, bf16[2,2,400,128]{3,2,1,0:T(8,128)(2,1)S(1)}, u32[]{:S(2)}, u32[]{:S(2)}) collective-permute-start(bf16[2,2,400,128]{3,2,1,0:T(8,128)(2,1)S(1)} %maximum_maximum_fusion.near), channel_id=1, source_target_pairs={{0,2},{1,3},{2,0},{3,1},{4,6},{5,7},{6,4},{7,5},{8,10},{9,11},{10,... | collective-permute-start | bytes 1228808 | tf_op jit(solution)/shard_map/ppermute | solution.py:431
